TPU v7x, 32 devices: a whole 2x2x4 slice. The times are simulated.
32 devices in a mesh: groups: 2 (over y), seq: 16 (over z, x, core).
Axes of the slice: x: 2, y: 2, z: 4, core: 2. Of those that a mesh axis runs over, the one named last changes fastest.
Arguments:
- key_values: bfloat16 [3, 2048, 8192], P(None, 'seq', 'groups'), parts along dimension 2, may hold values from -14 to 14, as said below
- bases: bfloat16 [3, 2, 1024, 256], replicated, may hold values from -0.1875 to 0.1875
- owner_slots: int32 [3, 64], P(None, ('groups', 'seq')), parts along dimension 1, may hold values from 0 to 15, as said below
Outputs:
- received: bfloat16 [512, 512, 128], P(('groups', 'seq')), parts along dimension 0
- grams: float32 [6, 2, 256, 256], P('groups'), parts along dimension 0
- energies: float32 [6, 2, 1024], P('groups'), parts along dimension 0
There are 2 independent parts, one for each index of `groups`. A program takes and returns all parts, laid end to end along the dimension named above; an argument that names none is the same for every part. Nothing has to cross between parts.
Inputs may be any that keep to these rules, and one draw needn't show every extreme that they name: key_values are finite real values within the range. `owner_slots`: block j of a layer belongs to device j // 2 of seq; the 6 values of one device's blocks over all layers are distinct, so an owner's slot is written at most once; some owner has all 16 slots filled.
All inputs are finite; a program needn't handle non-finite values.
Results may differ from a plain program's by a relative error of at most 0.001.
Values may be sent and summed in bfloat16 or wider, within the bound.
A program may use at most 128 MiB of HBM per device.

v0:
```python
import jax
import jax.numpy as jnp
from jax import lax
from jax.sharding import PartitionSpec as P

REACH = 8
OWNER_SLOT_LIMIT = 2
CAP = 16


def from_behind(block, axis, distance):
    devices = range(lax.axis_size(axis))
    route = [((i - distance) % len(devices), i) for i in devices]
    return lax.ppermute(block, axis, route)


def per_device(key_values, bases, owner_slots):
    dev_count = lax.axis_size("seq")
    layers = key_values.shape[0]
    width = bases.shape[2]
    rank = bases.shape[3]
    tok_dev = key_values.shape[2] // dev_count
    tokens = tok_dev * dev_count
    blk_dev = owner_slots.shape[1]
    blk_rows = tok_dev // blk_dev
    whole = lax.all_to_all(key_values, "seq", split_axis=2, concat_axis=1, tiled=True)
    gram_list = []
    energy_list = []
    block_list = []
    for layer_idx in range(layers):
        slab_rows = whole[layer_idx]
        slab_rows = slab_rows.reshape(2, width, tok_dev)
        basis = bases[layer_idx]
        coeff = jnp.einsum(
            "scr,sct->srt", basis, slab_rows, preferred_element_type=jnp.float32
        ).astype(jnp.bfloat16)
        recon = jnp.einsum("scr,srt->sct", basis, coeff, preferred_element_type=jnp.float32)
        resid = slab_rows.astype(jnp.float32) - recon
        energy_term = jnp.sum(resid * resid, axis=2)
        gram_term = jnp.einsum("srt,sqt->srq", coeff, coeff, preferred_element_type=jnp.float32)
        gram_total, energy_total = lax.psum((gram_term, energy_term), "seq")
        gram_list.append(gram_total / tokens)
        energy_list.append(energy_total / tokens)
        block_list.append(coeff.reshape(2 * rank, blk_dev, blk_rows).transpose(1, 0, 2))
    grams = jnp.stack(gram_list)
    energies = jnp.stack(energy_list)
    unit_count = layers * blk_dev
    units = jnp.stack(block_list).reshape(unit_count, 2 * rank * blk_rows)
    slot_vals = owner_slots.reshape(unit_count)
    one_hot = (slot_vals[:, None] == jnp.arange(CAP, dtype=jnp.int32)[None, :]).astype(jnp.bfloat16)
    outgoing = jnp.einsum("us,uf->sf", one_hot, units, preferred_element_type=jnp.float32).astype(
        jnp.bfloat16
    )
    outgoing = outgoing.reshape(REACH, OWNER_SLOT_LIMIT, 2 * rank, blk_rows)
    arrived = [outgoing[0]]
    for offset in range(1, REACH):
        arrived.append(from_behind(outgoing[offset], "seq", offset))
    buffer_all = jnp.stack(arrived)
    received = buffer_all.reshape(REACH * OWNER_SLOT_LIMIT, 2 * rank, blk_rows)
    return (received, grams, energies)


def solution(mesh):
    in_specs = (P(None, "seq", "groups"), P(), P(None, ("groups", "seq")))
    out_specs = (
        P(("groups", "seq"), None, None),
        P("groups", None, None, None),
        P("groups", None, None),
    )
    return jax.shard_map(
        per_device, mesh=mesh, in_specs=in_specs, out_specs=out_specs, check_vma=False
    )
```

profile of v0, /device:TPU:0, one launch (start us, length us, event | category | flops | bytes accessed | tf_op | source)
XLA Modules:
  0.0 329.7 jit_solution(11468838820563559150)
XLA Ops:
  7.2 7.2 %copy.39 = bf16[3,128,4096]{1,0,2:T(4,128)(2,1)} copy(bf16[3,128,4096]{2,1,0:T(8,128)(2,1)} %param.3) | data formatting | bytes 6291456 | tf_op args[0]
  14.4 7.5 %all-to-all-start = ((bf16[3,128,4096]{1,0,2:T(4,128)(2,1)}), bf16[3,128,4096]{1,0,2:T(4,128)(2,1)}, u32[]{:S(2)}, u32[]{:S(2)}) async-start(bf16[3,128,4096]{1,0,2:T(4,128)(2,1)} %copy.39), calls=%async_computation | async-start | bytes 8388608 | tf_op jit(solution)/shard_map/all_to_all | solution.py:26
  22.0 0.0 all-reduce.4.cloned.1.call-start
  22.0 0.1 copy.37
  22.1 0.1 eq.15
  22.2 77.4 %all-to-all-done = bf16[3,128,4096]{1,0,2:T(4,128)(2,1)} async-done(((bf16[3,128,4096]{1,0,2:T(4,128)(2,1)}), bf16[3,128,4096]{1,0,2:T(4,128)(2,1)}, u32[]{:S(2)}, u32[]{:S(2)}) %all-to-all-start) | async-done | bytes 3145760 | tf_op jit(solution)/shard_map/all_to_all | solution.py:26
  99.6 5.5 %copy.40 = bf16[3,128,16,256]{3,1,2,0:T(8,128)(2,1)S(1)} copy(bf16[3,128,16,256]{1,0,3,2:T(4,128)(2,1)} %bitcast.1) | data formatting | bytes 6291456 | tf_op jit(solution)/shard_map/all_to_all | solution.py:26
  105.2 1.6 fusion.21
  106.8 1.0 copy-done.4
  107.8 0.5 convolution_convert_fusion.2
  108.3 0.6 fusion.3
  108.9 0.1 reshape.45
  109.0 0.6 copy-done.1
  109.5 1.8 convolution_convert_fusion.1
  111.3 1.9 fusion.1
  113.2 0.1 reshape.46
  113.3 1.7 convolution_convert_fusion.3
  115.0 1.8 fusion.5
  116.8 0.1 reshape.44
  116.9 1.1 fusion.22
  118.0 1.1 fusion.23
  119.0 1.1 fusion.24
  120.1 0.1 copy_bitcast_fusion.7
  120.2 0.1 pad_maximum_fusion.1
  120.3 0.9 convolution_convert_fusion
  121.2 1.5 slice_bitcast_fusion
  122.8 0.7 bitcast_dynamic-update-slice_fusion
  123.5 0.8 collective-permute-start
  124.4 6.2 %collective-permute-start.1 = (bf16[2,512,128]{2,1,0:T(8,128)(2,1)S(1)}, bf16[2,512,128]{2,1,0:T(8,128)(2,1)S(1)}, u32[]{:S(2)}, u32[]{:S(2)}) collective-permute-start(bf16[2,512,128]{2,1,0:T(8,128)(2,1)S(1)} %bitcast.153), channel_id=1, source_target_pairs={{14,0},{15,1},{0,2},{1,3},{2,4},{3,5},{4,6},{5,7},{6,8},{7,9},{8,1... | collective-permute-start | bytes 786440 | tf_op jit(solution)/shard_map/ppermute | solution.py:14
  130.7 12.0 %collective-permute-start.2 = (bf16[2,512,128]{2,1,0:T(8,128)(2,1)S(1)}, bf16[2,512,128]{2,1,0:T(8,128)(2,1)S(1)}, u32[]{:S(2)}, u32[]{:S(2)}) collective-permute-start(bf16[2,512,128]{2,1,0:T(8,128)(2,1)S(1)} %bitcast.152), channel_id=1, source_target_pairs={{13,0},{14,1},{15,2},{0,3},{1,4},{2,5},{3,6},{4,7},{5,8},{6,9},{7,... | collective-permute-start | bytes 786440 | tf_op jit(solution)/shard_map/ppermute | solution.py:14
  142.7 0.7 collective-permute-start.3
  143.5 0.2 collective-permute-start.4
  143.6 75.5 %all-reduce = (f32[2,1024]{1,0:T(2,128)S(1)}, f32[2,1024]{1,0:T(2,128)S(1)}, f32[2,1024]{1,0:T(2,128)S(1)}) all-reduce(f32[2,1024]{1,0:T(2,128)S(1)} %fusion.1, f32[2,1024]{1,0:T(2,128)S(1)} %fusion.3, f32[2,1024]{1,0:T(2,128)S(1)} %fusion.5), channel_id=1, replica_groups=mesh['groups'=2,'seq'=16] {'seq'}, use_global_device_ids=true, to_apply=%region_8.0 | all-reduce | flops 6144 | bytes 49152 | tf_op jit(solution)/shard_map/psum | solution.py:41
  219.1 0.6 pad_maximum_fusion.2
  219.9 0.0 all-reduce.4.cloned.1.call-update
  219.9 0.1 collective-permute-start.5
  220.0 0.7 bitcast_dynamic-update-slice_fusion.7
  220.7 0.7 bitcast_dynamic-update-slice_fusion.6
  221.4 0.7 bitcast_dynamic-update-slice_fusion.5
  222.1 0.7 bitcast_dynamic-update-slice_fusion.4
  222.9 0.7 bitcast_dynamic-update-slice_fusion.3
  223.6 16.2 %collective-permute-done.5 = bf16[2,512,128]{2,1,0:T(8,128)(2,1)S(1)} collective-permute-done((bf16[2,512,128]{2,1,0:T(8,128)(2,1)S(1)}, bf16[2,512,128]{2,1,0:T(8,128)(2,1)S(1)}, u32[]{:S(2)}, u32[]{:S(2)}) %collective-permute-start.5) | collective-permute-done | bytes 262176 | tf_op jit(solution)/shard_map/ppermute | solution.py:14
  239.8 0.7 bitcast_dynamic-update-slice_fusion.2
  240.5 0.7 bitcast_dynamic-update-slice_fusion.1
  241.2 78.0 %all-reduce.4.cloned.1.call-done = (f32[2,256,256]{2,1,0:T(8,128)}, f32[2,256,256]{2,1,0:T(8,128)}, f32[2,256,256]{2,1,0:T(8,128)}) async-done(((f32[2,256,256]{2,1,0:T(8,128)}, f32[2,256,256]{2,1,0:T(8,128)}, f32[2,256,256]{2,1,0:T(8,128)}), (f32[2,256,256]{2,1,0:T(8,128)}, f32[2,256,256]{2,1,0:T(8,128)}, f32[2,256,256]{2,1,0:T(8,128)})) %all-reduce.4.cloned.1.call-update) | async-done | bytes 1572880 | tf_op jit(solution)/shard_map/psum | solution.py:41
  319.2 1.1 multiply_bitcast_fusion.2
  320.3 1.3 multiply_bitcast_fusion
  321.6 1.2 pad_maximum_fusion
  (25 shorter events, 0.3 us)
Async XLA Ops:
  14.4 7.6 %copy-start.3 = (s32[3,2]{0,1:T(2,128)S(1)}, s32[3,2]{0,1:T(2,128)}, u32[]{:S(2)}) copy-start(s32[3,2]{0,1:T(2,128)} %param.5) | copy-start | bytes 76
  14.4 85.2 %all-to-all-start = ((bf16[3,128,4096]{1,0,2:T(4,128)(2,1)}), bf16[3,128,4096]{1,0,2:T(4,128)(2,1)}, u32[]{:S(2)}, u32[]{:S(2)}) async-start(bf16[3,128,4096]{1,0,2:T(4,128)(2,1)} %copy.39), calls=%async_computation | async-start | bytes 8388608 | tf_op jit(solution)/shard_map/all_to_all | solution.py:26
  22.0 297.3 %all-reduce.4.cloned.1.call-start = ((), (), s32[]{:S(2)}) async-start(), calls=%async_computation.1 | async-start | bytes 3145728 | tf_op jit(solution)/shard_map/psum | solution.py:41
  105.1 2.6 copy-start.4
  108.3 1.2 copy-start.1
  109.0 2.3 copy-start.2
  111.3 2.0 copy-start
  123.5 96.4 %collective-permute-start = (bf16[2,512,128]{2,1,0:T(8,128)(2,1)S(1)}, bf16[2,512,128]{2,1,0:T(8,128)(2,1)S(1)}, u32[]{:S(2)}, u32[]{:S(2)}) collective-permute-start(bf16[2,512,128]{2,1,0:T(8,128)(2,1)S(1)} %bitcast.154), channel_id=1, source_target_pairs={{15,0},{0,1},{1,2},{2,3},{3,4},{4,5},{5,6},{6,7},{7,8},{8,9},{9,10... | collective-permute-start | bytes 786440 | tf_op jit(solution)/shard_map/ppermute | solution.py:14
  124.4 96.3 %collective-permute-start.1 = (bf16[2,512,128]{2,1,0:T(8,128)(2,1)S(1)}, bf16[2,512,128]{2,1,0:T(8,128)(2,1)S(1)}, u32[]{:S(2)}, u32[]{:S(2)}) collective-permute-start(bf16[2,512,128]{2,1,0:T(8,128)(2,1)S(1)} %bitcast.153), channel_id=1, source_target_pairs={{14,0},{15,1},{0,2},{1,3},{2,4},{3,5},{4,6},{5,7},{6,8},{7,9},{8,1... | collective-permute-start | bytes 786440 | tf_op jit(solution)/shard_map/ppermute | solution.py:14
  130.7 90.7 %collective-permute-start.2 = (bf16[2,512,128]{2,1,0:T(8,128)(2,1)S(1)}, bf16[2,512,128]{2,1,0:T(8,128)(2,1)S(1)}, u32[]{:S(2)}, u32[]{:S(2)}) collective-permute-start(bf16[2,512,128]{2,1,0:T(8,128)(2,1)S(1)} %bitcast.152), channel_id=1, source_target_pairs={{13,0},{14,1},{15,2},{0,3},{1,4},{2,5},{3,6},{4,7},{5,8},{6,9},{7,... | collective-permute-start | bytes 786440 | tf_op jit(solution)/shard_map/ppermute | solution.py:14
  142.7 79.4 %collective-permute-start.3 = (bf16[2,512,128]{2,1,0:T(8,128)(2,1)S(1)}, bf16[2,512,128]{2,1,0:T(8,128)(2,1)S(1)}, u32[]{:S(2)}, u32[]{:S(2)}) collective-permute-start(bf16[2,512,128]{2,1,0:T(8,128)(2,1)S(1)} %bitcast.151), channel_id=1, source_target_pairs={{12,0},{13,1},{14,2},{15,3},{0,4},{1,5},{2,6},{3,7},{4,8},{5,9},{6... | collective-permute-start | bytes 786440 | tf_op jit(solution)/shard_map/ppermute | solution.py:14
  143.5 79.4 %collective-permute-start.4 = (bf16[2,512,128]{2,1,0:T(8,128)(2,1)S(1)}, bf16[2,512,128]{2,1,0:T(8,128)(2,1)S(1)}, u32[]{:S(2)}, u32[]{:S(2)}) collective-permute-start(bf16[2,512,128]{2,1,0:T(8,128)(2,1)S(1)} %bitcast.150), channel_id=1, source_target_pairs={{11,0},{12,1},{13,2},{14,3},{15,4},{0,5},{1,6},{2,7},{3,8},{4,9},{... | collective-permute-start | bytes 786440 | tf_op jit(solution)/shard_map/ppermute | solution.py:14
  219.9 19.9 %collective-permute-start.5 = (bf16[2,512,128]{2,1,0:T(8,128)(2,1)S(1)}, bf16[2,512,128]{2,1,0:T(8,128)(2,1)S(1)}, u32[]{:S(2)}, u32[]{:S(2)}) collective-permute-start(bf16[2,512,128]{2,1,0:T(8,128)(2,1)S(1)} %bitcast.156), channel_id=1, source_target_pairs={{10,0},{11,1},{12,2},{13,3},{14,4},{15,5},{0,6},{1,7},{2,8},{3,9},... | collective-permute-start | bytes 786440 | tf_op jit(solution)/shard_map/ppermute | solution.py:14
  220.7 19.8 %collective-permute-start.6 = (bf16[2,512,128]{2,1,0:T(8,128)(2,1)S(1)}, bf16[2,512,128]{2,1,0:T(8,128)(2,1)S(1)}, u32[]{:S(2)}, u32[]{:S(2)}) collective-permute-start(bf16[2,512,128]{2,1,0:T(8,128)(2,1)S(1)} %bitcast.155), channel_id=1, source_target_pairs={{9,0},{10,1},{11,2},{12,3},{13,4},{14,5},{15,6},{0,7},{1,8},{2,9},... | collective-permute-start | bytes 786440 | tf_op jit(solution)/shard_map/ppermute | solution.py:14
Sparse Core Ops, SparseCore 0:
  220.0 99.1 all-reduce.3
where the time goes:
time: 330 us
  waiting for transfers between devices  172 us (52%)
  blocking collectives  75.5 us (23%)
  starting transfers between devices  27.6 us (8%)
  local copies, waits for them, and re-layouts  24 us (7%)
  between operations  14.3 us (4%)
  matrix products  12.3 us (4%)
  other arithmetic  4.34 us (1%)
    psum x1, waiting for transfers between devices, per_device(): gram_total, energy_total = lax.psum((gram_term, energy_term), 'seq')  78 us
    all_to_all x1, waiting for transfers between devices, per_device(): lax.all_to_all(key_values, 'seq', split_axis=2, concat_axis=1, tiled=True)  77.4 us
    psum x1, blocking collectives, per_device(): gram_total, energy_total = lax.psum((gram_term, energy_term), 'seq')  75.5 us
    ppermute x7, starting transfers between devices, from_behind(): return lax.ppermute(block, axis, route)  20 us
    ppermute x7, waiting for transfers between devices, from_behind(): return lax.ppermute(block, axis, route)  16.2 us
    unnamed x27, local copies, waits for them, and re-layouts  15.8 us
    all_to_all x1, starting transfers between devices, per_device(): lax.all_to_all(key_values, 'seq', split_axis=2, concat_axis=1, tiled=True)  7.54 us
  transfers between devices with their start and end apart: 9, of which 3 were waited for; matrix products, arithmetic and copies ran while one was open for 2% of the time, Pallas kernels for 0%

commit v1 on v0

--- a/solution.py
+++ b/solution.py
@@ -6,6 +6,18 @@
 REACH = 8
 OWNER_SLOT_LIMIT = 2
 CAP = 16
+
+
+def exchange_directly(shard, axis, split, join):
+    ways, here = (lax.axis_size(axis), lax.axis_index(axis))
+    width = shard.shape[split] // ways
+    turned = jnp.roll(shard, -here * width, axis=split)
+    got = [lax.slice_in_dim(turned, 0, width, axis=split)]
+    for far in range(1, ways):
+        sent = lax.slice_in_dim(turned, far * width, (far + 1) * width, axis=split)
+        got.append(lax.ppermute(sent, axis, [(d, (d + far) % ways) for d in range(ways)]))
+    line = jnp.concatenate(got[::-1], axis=join)
+    return jnp.roll(line, (here + 1) * got[0].shape[join], axis=join)
 
 
 def from_behind(block, axis, distance):
@@ -23,7 +35,7 @@
     tokens = tok_dev * dev_count
     blk_dev = owner_slots.shape[1]
     blk_rows = tok_dev // blk_dev
-    whole = lax.all_to_all(key_values, "seq", split_axis=2, concat_axis=1, tiled=True)
+    whole = exchange_directly(key_values, "seq", 2, 1)
     gram_list = []
     energy_list = []
     block_list = []

time: 330 us -> 314 us (0.952)
  waiting for transfers between devices: 172 us -> 144 us
  starting transfers between devices: 27.6 us -> 33.3 us
  local copies, waits for them, and re-layouts: 24 us -> 19.5 us
  other arithmetic: 4.34 us -> 8.75 us
    all_to_all x1 -> x0, waiting for transfers between devices: 77.4 us -> none  [per_device(): lax.all_to_all(key_values, 'seq', split_axis=2, concat_axis=1, tiled=True)]
    ppermute x0 -> x15, waiting for transfers between devices: none -> 49.3 us  [exchange_directly(): lax.ppermute(sent, axis, [(d, (d + far) % ways) for d in range(ways)])]
    ppermute x0 -> x15, starting transfers between devices: none -> 29.7 us  [exchange_directly(): lax.ppermute(sent, axis, [(d, (d + far) % ways) for d in range(ways)])]
    ppermute x7, starting transfers between devices: 20 us -> 3.5 us  [from_behind(): return lax.ppermute(block, axis, route)]
    all_to_all x1 -> x0, starting transfers between devices: 7.54 us -> none  [per_device(): lax.all_to_all(key_values, 'seq', split_axis=2, concat_axis=1, tiled=True)]
    all_to_all x1 -> x0, local copies, waits for them, and re-layouts: 5.5 us -> none  [per_device(): lax.all_to_all(key_values, 'seq', split_axis=2, concat_axis=1, tiled=True)]
    unnamed x27 -> x51, local copies, waits for them, and re-layouts: 15.8 us -> 13 us
  transfers between devices with their start and end apart: 9 -> 23, of which waited for: 3 -> 12; matrix products, arithmetic and copies ran while one was open for 2% -> 3% of each run, Pallas kernels for 0% -> 0%
where the time goes in v1:
time: 314 us; the launch traced here: 313 us
  waiting for transfers between devices  144 us (46%)
  blocking collectives  78.2 us (25%)
  starting transfers between devices  33.3 us (11%)
  local copies, waits for them, and re-layouts  19.5 us (6%)
  matrix products  15 us (5%)
  between operations  14.6 us (5%)
  other arithmetic  8.75 us (3%)
    psum x1, waiting for transfers between devices, per_device(): gram_total, energy_total = lax.psum((gram_term, energy_term), 'seq')  78.2 us
    psum x1, blocking collectives, per_device(): gram_total, energy_total = lax.psum((gram_term, energy_term), 'seq')  78.2 us
    ppermute x15, waiting for transfers between devices, exchange_directly(): lax.ppermute(sent, axis, [(d, (d + far) % ways) for d in range(ways)])  49.3 us
    ppermute x15, starting transfers between devices, exchange_directly(): lax.ppermute(sent, axis, [(d, (d + far) % ways) for d in range(ways)])  29.7 us
    ppermute x7, waiting for transfers between devices, from_behind(): return lax.ppermute(block, axis, route)  16.1 us
    unnamed x51, local copies, waits for them, and re-layouts  13 us
  transfers between devices with their start and end apart: 23, of which 12 were waited for; matrix products, arithmetic and copies ran while one was open for 3% of the time, Pallas kernels for 0%

profile of v1, /device:TPU:0, one launch (start us, length us, event | category | flops | bytes accessed | tf_op | source)
XLA Modules:
  0.0 313.0 jit_solution(9255597524868453331)
XLA Ops:
  7.2 3.2 %fusion = bf16[3,128,4096]{2,1,0:T(8,128)(2,1)S(1)} fusion(s32[]{:T(128)S(6)} %select_n.24, bf16[3,128,4096]{2,1,0:T(8,128)(2,1)} %param.3), kind=kLoop, calls=%fused_computation.3 | loop fusion | flops 6291456 | bytes 6291460 | tf_op jit(solution)/shard_map/jit(_roll_dynamic)/concatenate | solution.py:14
  10.5 1.6 fusion.25
  12.1 5.5 %collective-permute-start = (bf16[3,128,256]{2,1,0:T(8,128)(2,1)}, bf16[3,128,256]{2,1,0:T(8,128)(2,1)S(1)}, u32[]{:S(2)}, u32[]{:S(2)}) collective-permute-start(bf16[3,128,256]{2,1,0:T(8,128)(2,1)} %get-tuple-element.26), channel_id=1, source_target_pairs={{0,15},{1,0},{2,1},{3,2},{4,3},{5,4},{6,5},{7,6},{8,7},{9,8},{10,9... | collective-permute-start | bytes 589832 | tf_op jit(solution)/shard_map/ppermute | solution.py:18
  19.0 4.2 %collective-permute-done = bf16[3,128,256]{2,1,0:T(8,128)(2,1)S(1)} collective-permute-done((bf16[3,128,256]{2,1,0:T(8,128)(2,1)}, bf16[3,128,256]{2,1,0:T(8,128)(2,1)S(1)}, u32[]{:S(2)}, u32[]{:S(2)}) %collective-permute-start) | collective-permute-done | bytes 196640 | tf_op jit(solution)/shard_map/ppermute | solution.py:18
  23.5 3.9 %collective-permute-done.1 = bf16[3,128,256]{2,1,0:T(8,128)(2,1)S(1)} collective-permute-done((bf16[3,128,256]{2,1,0:T(8,128)(2,1)}, bf16[3,128,256]{2,1,0:T(8,128)(2,1)S(1)}, u32[]{:S(2)}, u32[]{:S(2)}) %collective-permute-start.1) | collective-permute-done | bytes 196640 | tf_op jit(solution)/shard_map/ppermute | solution.py:18
  27.4 4.2 %collective-permute-done.2 = bf16[3,128,256]{2,1,0:T(8,128)(2,1)} collective-permute-done((bf16[3,128,256]{2,1,0:T(8,128)(2,1)}, bf16[3,128,256]{2,1,0:T(8,128)(2,1)}, u32[]{:S(2)}, u32[]{:S(2)}) %collective-permute-start.2) | collective-permute-done | bytes 196640 | tf_op jit(solution)/shard_map/ppermute | solution.py:18
  31.6 0.9 constant_dynamic-update-slice_fusion.27
  32.5 3.3 %collective-permute-done.3 = bf16[3,128,256]{2,1,0:T(8,128)(2,1)} collective-permute-done((bf16[3,128,256]{2,1,0:T(8,128)(2,1)}, bf16[3,128,256]{2,1,0:T(8,128)(2,1)}, u32[]{:S(2)}, u32[]{:S(2)}) %collective-permute-start.3) | collective-permute-done | bytes 196640 | tf_op jit(solution)/shard_map/ppermute | solution.py:18
  35.8 0.9 constant_dynamic-update-slice_fusion.26
  36.7 3.3 %collective-permute-done.4 = bf16[3,128,256]{2,1,0:T(8,128)(2,1)} collective-permute-done((bf16[3,128,256]{2,1,0:T(8,128)(2,1)}, bf16[3,128,256]{2,1,0:T(8,128)(2,1)}, u32[]{:S(2)}, u32[]{:S(2)}) %collective-permute-start.4) | collective-permute-done | bytes 196640 | tf_op jit(solution)/shard_map/ppermute | solution.py:18
  40.0 0.9 constant_dynamic-update-slice_fusion.25
  40.9 3.3 %collective-permute-done.5 = bf16[3,128,256]{2,1,0:T(8,128)(2,1)S(1)} collective-permute-done((bf16[3,128,256]{2,1,0:T(8,128)(2,1)}, bf16[3,128,256]{2,1,0:T(8,128)(2,1)S(1)}, u32[]{:S(2)}, u32[]{:S(2)}) %collective-permute-start.5) | collective-permute-done | bytes 196640 | tf_op jit(solution)/shard_map/ppermute | solution.py:18
  44.2 13.9 %collective-permute-start.10 = (bf16[3,128,256]{2,1,0:T(8,128)(2,1)}, bf16[3,128,256]{2,1,0:T(8,128)(2,1)S(1)}, u32[]{:S(2)}, u32[]{:S(2)}) collective-permute-start(bf16[3,128,256]{2,1,0:T(8,128)(2,1)} %get-tuple-element.16), channel_id=1, source_target_pairs={{0,5},{1,6},{2,7},{3,8},{4,9},{5,10},{6,11},{7,12},{8,13},{9,14},{... | collective-permute-start | bytes 589832 | tf_op jit(solution)/shard_map/ppermute | solution.py:18
  58.2 8.5 %collective-permute-start.11 = (bf16[3,128,256]{2,1,0:T(8,128)(2,1)}, bf16[3,128,256]{2,1,0:T(8,128)(2,1)S(1)}, u32[]{:S(2)}, u32[]{:S(2)}) collective-permute-start(bf16[3,128,256]{2,1,0:T(8,128)(2,1)} %get-tuple-element.15), channel_id=1, source_target_pairs={{0,4},{1,5},{2,6},{3,7},{4,8},{5,9},{6,10},{7,11},{8,12},{9,13},{1... | collective-permute-start | bytes 589832 | tf_op jit(solution)/shard_map/ppermute | solution.py:18
  66.7 17.2 %collective-permute-done.7 = bf16[3,128,256]{2,1,0:T(8,128)(2,1)S(1)} collective-permute-done((bf16[3,128,256]{2,1,0:T(8,128)(2,1)}, bf16[3,128,256]{2,1,0:T(8,128)(2,1)S(1)}, u32[]{:S(2)}, u32[]{:S(2)}) %collective-permute-start.7) | collective-permute-done | bytes 196640 | tf_op jit(solution)/shard_map/ppermute | solution.py:18
  84.4 6.6 %collective-permute-done.12 = bf16[3,128,256]{2,1,0:T(8,128)(2,1)S(1)} collective-permute-done((bf16[3,128,256]{2,1,0:T(8,128)(2,1)}, bf16[3,128,256]{2,1,0:T(8,128)(2,1)S(1)}, u32[]{:S(2)}, u32[]{:S(2)}) %collective-permute-start.12) | collective-permute-done | bytes 196640 | tf_op jit(solution)/shard_map/ppermute | solution.py:18
  91.0 3.4 %collective-permute-done.13 = bf16[3,128,256]{2,1,0:T(8,128)(2,1)S(1)} collective-permute-done((bf16[3,128,256]{2,1,0:T(8,128)(2,1)}, bf16[3,128,256]{2,1,0:T(8,128)(2,1)S(1)}, u32[]{:S(2)}, u32[]{:S(2)}) %collective-permute-start.13) | collective-permute-done | bytes 196640 | tf_op jit(solution)/shard_map/ppermute | solution.py:18
  94.5 0.9 constant_dynamic-update-slice_fusion.12
  95.5 0.9 constant_dynamic-update-slice_fusion.11
  96.4 0.9 constant_dynamic-update-slice_fusion.10
  97.8 1.3 copy.21
  99.2 1.7 convolution_convert_fusion.3
  100.9 1.3 copy.22
  102.2 1.7 convolution_convert_fusion.2
  104.5 1.8 convolution_convert_fusion.1
  106.4 1.1 fusion.26
  107.4 2.0 fusion.6
  109.5 1.1 fusion.27
  110.6 1.7 fusion.4
  112.3 1.1 fusion.28
  113.4 1.7 fusion.2
  115.8 1.3 pad_maximum_fusion.1
  117.2 0.9 convolution_convert_fusion
  118.1 1.5 slice_bitcast_fusion
  119.7 0.7 bitcast_dynamic-update-slice_fusion
  121.3 1.8 collective-permute-start.18
  123.1 0.9 collective-permute-start.19
  124.1 78.2 %all-reduce = (f32[2,1024]{1,0:T(2,128)S(1)}, f32[2,1024]{1,0:T(2,128)S(1)}, f32[2,1024]{1,0:T(2,128)S(1)}) all-reduce(f32[2,1024]{1,0:T(2,128)S(1)} %fusion.2, f32[2,1024]{1,0:T(2,128)S(1)} %fusion.4, f32[2,1024]{1,0:T(2,128)S(1)} %fusion.6), channel_id=1, replica_groups=mesh['groups'=2,'seq'=16] {'seq'}, use_global_device_ids=true, to_apply=%region_8.9 | all-reduce | flops 6144 | bytes 49152 | tf_op jit(solution)/shard_map/psum | solution.py:53
  203.1 0.7 bitcast_dynamic-update-slice_fusion.7
  203.8 0.7 bitcast_dynamic-update-slice_fusion.6
  204.5 0.7 bitcast_dynamic-update-slice_fusion.5
  205.3 0.7 bitcast_dynamic-update-slice_fusion.4
  206.7 16.1 %collective-permute-done.20 = bf16[2,512,128]{2,1,0:T(8,128)(2,1)S(1)} collective-permute-done((bf16[2,512,128]{2,1,0:T(8,128)(2,1)S(1)}, bf16[2,512,128]{2,1,0:T(8,128)(2,1)S(1)}, u32[]{:S(2)}, u32[]{:S(2)}) %collective-permute-start.20) | collective-permute-done | bytes 262176 | tf_op jit(solution)/shard_map/ppermute | solution.py:26
  223.5 0.7 bitcast_dynamic-update-slice_fusion.1
  224.2 78.2 %all-reduce.4.cloned.1.call-done = (f32[2,256,256]{2,1,0:T(8,128)}, f32[2,256,256]{2,1,0:T(8,128)}, f32[2,256,256]{2,1,0:T(8,128)}) async-done(((f32[2,256,256]{2,1,0:T(8,128)}, f32[2,256,256]{2,1,0:T(8,128)}, f32[2,256,256]{2,1,0:T(8,128)}), (f32[2,256,256]{2,1,0:T(8,128)}, f32[2,256,256]{2,1,0:T(8,128)}, f32[2,256,256]{2,1,0:T(8,128)})) %all-reduce.4.cloned.1.call-update) | async-done | bytes 1572880 | tf_op jit(solution)/shard_map/psum | solution.py:53
  302.5 1.1 multiply_bitcast_fusion.2
  303.6 1.3 multiply_bitcast_fusion
  304.9 1.2 pad_maximum_fusion
  (84 shorter events, 7.2 us)
Async XLA Ops:
  7.2 11.6 %copy-start.1 = (s32[3,2]{0,1:T(2,128)S(1)}, s32[3,2]{0,1:T(2,128)}, u32[]{:S(2)}) copy-start(s32[3,2]{0,1:T(2,128)} %param.5) | copy-start | bytes 76
  7.2 295.3 %all-reduce.4.cloned.1.call-start = ((), (), s32[]{:S(2)}) async-start(), calls=%async_computation | async-start | bytes 3145728 | tf_op jit(solution)/shard_map/psum | solution.py:53
  12.1 11.1 %collective-permute-start = (bf16[3,128,256]{2,1,0:T(8,128)(2,1)}, bf16[3,128,256]{2,1,0:T(8,128)(2,1)S(1)}, u32[]{:S(2)}, u32[]{:S(2)}) collective-permute-start(bf16[3,128,256]{2,1,0:T(8,128)(2,1)} %get-tuple-element.26), channel_id=1, source_target_pairs={{0,15},{1,0},{2,1},{3,2},{4,3},{5,4},{6,5},{7,6},{8,7},{9,8},{10,9... | collective-permute-start | bytes 589832 | tf_op jit(solution)/shard_map/ppermute | solution.py:18
  17.6 9.8 %collective-permute-start.1 = (bf16[3,128,256]{2,1,0:T(8,128)(2,1)}, bf16[3,128,256]{2,1,0:T(8,128)(2,1)S(1)}, u32[]{:S(2)}, u32[]{:S(2)}) collective-permute-start(bf16[3,128,256]{2,1,0:T(8,128)(2,1)} %get-tuple-element.25), channel_id=1, source_target_pairs={{0,14},{1,15},{2,0},{3,1},{4,2},{5,3},{6,4},{7,5},{8,6},{9,7},{10,... | collective-permute-start | bytes 589832 | tf_op jit(solution)/shard_map/ppermute | solution.py:18
  18.1 13.5 %collective-permute-start.2 = (bf16[3,128,256]{2,1,0:T(8,128)(2,1)}, bf16[3,128,256]{2,1,0:T(8,128)(2,1)}, u32[]{:S(2)}, u32[]{:S(2)}) collective-permute-start(bf16[3,128,256]{2,1,0:T(8,128)(2,1)} %get-tuple-element.24), channel_id=1, source_target_pairs={{0,13},{1,14},{2,15},{3,0},{4,1},{5,2},{6,3},{7,4},{8,5},{9,6},{10... | collective-permute-start | bytes 589832 | tf_op jit(solution)/shard_map/ppermute | solution.py:18
  18.4 17.4 %collective-permute-start.3 = (bf16[3,128,256]{2,1,0:T(8,128)(2,1)}, bf16[3,128,256]{2,1,0:T(8,128)(2,1)}, u32[]{:S(2)}, u32[]{:S(2)}) collective-permute-start(bf16[3,128,256]{2,1,0:T(8,128)(2,1)} %get-tuple-element.23), channel_id=1, source_target_pairs={{0,12},{1,13},{2,14},{3,15},{4,0},{5,1},{6,2},{7,3},{8,4},{9,5},{1... | collective-permute-start | bytes 589832 | tf_op jit(solution)/shard_map/ppermute | solution.py:18
  18.8 21.2 %collective-permute-start.4 = (bf16[3,128,256]{2,1,0:T(8,128)(2,1)}, bf16[3,128,256]{2,1,0:T(8,128)(2,1)}, u32[]{:S(2)}, u32[]{:S(2)}) collective-permute-start(bf16[3,128,256]{2,1,0:T(8,128)(2,1)} %get-tuple-element.22), channel_id=1, source_target_pairs={{0,11},{1,12},{2,13},{3,14},{4,15},{5,0},{6,1},{7,2},{8,3},{9,4},{... | collective-permute-start | bytes 589832 | tf_op jit(solution)/shard_map/ppermute | solution.py:18
  23.1 21.1 %collective-permute-start.5 = (bf16[3,128,256]{2,1,0:T(8,128)(2,1)}, bf16[3,128,256]{2,1,0:T(8,128)(2,1)S(1)}, u32[]{:S(2)}, u32[]{:S(2)}) collective-permute-start(bf16[3,128,256]{2,1,0:T(8,128)(2,1)} %get-tuple-element.21), channel_id=1, source_target_pairs={{0,10},{1,11},{2,12},{3,13},{4,14},{5,15},{6,0},{7,1},{8,2},{9,3},... | collective-permute-start | bytes 589832 | tf_op jit(solution)/shard_map/ppermute | solution.py:18
  27.4 30.8 %collective-permute-start.6 = (bf16[3,128,256]{2,1,0:T(8,128)(2,1)}, bf16[3,128,256]{2,1,0:T(8,128)(2,1)S(1)}, u32[]{:S(2)}, u32[]{:S(2)}) collective-permute-start(bf16[3,128,256]{2,1,0:T(8,128)(2,1)} %get-tuple-element.20), channel_id=1, source_target_pairs={{0,9},{1,10},{2,11},{3,12},{4,13},{5,14},{6,15},{7,0},{8,1},{9,2},... | collective-permute-start | bytes 589832 | tf_op jit(solution)/shard_map/ppermute | solution.py:18
  31.6 52.3 %collective-permute-start.7 = (bf16[3,128,256]{2,1,0:T(8,128)(2,1)}, bf16[3,128,256]{2,1,0:T(8,128)(2,1)S(1)}, u32[]{:S(2)}, u32[]{:S(2)}) collective-permute-start(bf16[3,128,256]{2,1,0:T(8,128)(2,1)} %get-tuple-element.19), channel_id=1, source_target_pairs={{0,8},{1,9},{2,10},{3,11},{4,12},{5,13},{6,14},{7,15},{8,0},{9,1},... | collective-permute-start | bytes 589832 | tf_op jit(solution)/shard_map/ppermute | solution.py:18
  35.8 48.2 %collective-permute-start.8 = (bf16[3,128,256]{2,1,0:T(8,128)(2,1)}, bf16[3,128,256]{2,1,0:T(8,128)(2,1)S(1)}, u32[]{:S(2)}, u32[]{:S(2)}) collective-permute-start(bf16[3,128,256]{2,1,0:T(8,128)(2,1)} %get-tuple-element.18), channel_id=1, source_target_pairs={{0,7},{1,8},{2,9},{3,10},{4,11},{5,12},{6,13},{7,14},{8,15},{9,0},... | collective-permute-start | bytes 589832 | tf_op jit(solution)/shard_map/ppermute | solution.py:18
  40.0 44.0 %collective-permute-start.9 = (bf16[3,128,256]{2,1,0:T(8,128)(2,1)}, bf16[3,128,256]{2,1,0:T(8,128)(2,1)S(1)}, u32[]{:S(2)}, u32[]{:S(2)}) collective-permute-start(bf16[3,128,256]{2,1,0:T(8,128)(2,1)} %get-tuple-element.17), channel_id=1, source_target_pairs={{0,6},{1,7},{2,8},{3,9},{4,10},{5,11},{6,12},{7,13},{8,14},{9,15},... | collective-permute-start | bytes 589832 | tf_op jit(solution)/shard_map/ppermute | solution.py:18
  44.2 40.1 %collective-permute-start.10 = (bf16[3,128,256]{2,1,0:T(8,128)(2,1)}, bf16[3,128,256]{2,1,0:T(8,128)(2,1)S(1)}, u32[]{:S(2)}, u32[]{:S(2)}) collective-permute-start(bf16[3,128,256]{2,1,0:T(8,128)(2,1)} %get-tuple-element.16), channel_id=1, source_target_pairs={{0,5},{1,6},{2,7},{3,8},{4,9},{5,10},{6,11},{7,12},{8,13},{9,14},{... | collective-permute-start | bytes 589832 | tf_op jit(solution)/shard_map/ppermute | solution.py:18
  58.2 26.2 %collective-permute-start.11 = (bf16[3,128,256]{2,1,0:T(8,128)(2,1)}, bf16[3,128,256]{2,1,0:T(8,128)(2,1)S(1)}, u32[]{:S(2)}, u32[]{:S(2)}) collective-permute-start(bf16[3,128,256]{2,1,0:T(8,128)(2,1)} %get-tuple-element.15), channel_id=1, source_target_pairs={{0,4},{1,5},{2,6},{3,7},{4,8},{5,9},{6,10},{7,11},{8,12},{9,13},{1... | collective-permute-start | bytes 589832 | tf_op jit(solution)/shard_map/ppermute | solution.py:18
  83.9 7.1 %collective-permute-start.12 = (bf16[3,128,256]{2,1,0:T(8,128)(2,1)}, bf16[3,128,256]{2,1,0:T(8,128)(2,1)S(1)}, u32[]{:S(2)}, u32[]{:S(2)}) collective-permute-start(bf16[3,128,256]{2,1,0:T(8,128)(2,1)} %get-tuple-element.14), channel_id=1, source_target_pairs={{0,3},{1,4},{2,5},{3,6},{4,7},{5,8},{6,9},{7,10},{8,11},{9,12},{10... | collective-permute-start | bytes 589832 | tf_op jit(solution)/shard_map/ppermute | solution.py:18
  84.0 10.4 %collective-permute-start.13 = (bf16[3,128,256]{2,1,0:T(8,128)(2,1)}, bf16[3,128,256]{2,1,0:T(8,128)(2,1)S(1)}, u32[]{:S(2)}, u32[]{:S(2)}) collective-permute-start(bf16[3,128,256]{2,1,0:T(8,128)(2,1)} %get-tuple-element.13), channel_id=1, source_target_pairs={{0,2},{1,3},{2,4},{3,5},{4,6},{5,7},{6,8},{7,9},{8,10},{9,11},{10,... | collective-permute-start | bytes 589832 | tf_op jit(solution)/shard_map/ppermute | solution.py:18
  84.0 10.4 %collective-permute-start.14 = (bf16[3,128,256]{2,1,0:T(8,128)(2,1)}, bf16[3,128,256]{2,1,0:T(8,128)(2,1)S(1)}, u32[]{:S(2)}, u32[]{:S(2)}) collective-permute-start(bf16[3,128,256]{2,1,0:T(8,128)(2,1)} %get-tuple-element.12), channel_id=1, source_target_pairs={{0,1},{1,2},{2,3},{3,4},{4,5},{5,6},{6,7},{7,8},{8,9},{9,10},{10,1... | collective-permute-start | bytes 589832 | tf_op jit(solution)/shard_map/ppermute | solution.py:18
  104.5 6.1 %copy-start = (bf16[2,1024,256]{1,2,0:T(8,128)(2,1)S(1)}, bf16[2,1024,256]{1,2,0:T(8,128)(2,1)}, u32[]{:S(2)}) copy-start(bf16[2,1024,256]{1,2,0:T(8,128)(2,1)} %copy.22) | copy-start | bytes 3145732
  120.4 82.6 %collective-permute-start.15 = (bf16[2,512,128]{2,1,0:T(8,128)(2,1)S(1)}, bf16[2,512,128]{2,1,0:T(8,128)(2,1)S(1)}, u32[]{:S(2)}, u32[]{:S(2)}) collective-permute-start(bf16[2,512,128]{2,1,0:T(8,128)(2,1)S(1)} %bitcast.155), channel_id=1, source_target_pairs={{15,0},{0,1},{1,2},{2,3},{3,4},{4,5},{5,6},{6,7},{7,8},{8,9},{9,10... | collective-permute-start | bytes 786440 | tf_op jit(solution)/shard_map/ppermute | solution.py:26
  120.5 83.3 %collective-permute-start.16 = (bf16[2,512,128]{2,1,0:T(8,128)(2,1)S(1)}, bf16[2,512,128]{2,1,0:T(8,128)(2,1)S(1)}, u32[]{:S(2)}, u32[]{:S(2)}) collective-permute-start(bf16[2,512,128]{2,1,0:T(8,128)(2,1)S(1)} %bitcast.154), channel_id=1, source_target_pairs={{14,0},{15,1},{0,2},{1,3},{2,4},{3,5},{4,6},{5,7},{6,8},{7,9},{8,1... | collective-permute-start | bytes 786440 | tf_op jit(solution)/shard_map/ppermute | solution.py:26
  120.7 83.9 %collective-permute-start.17 = (bf16[2,512,128]{2,1,0:T(8,128)(2,1)S(1)}, bf16[2,512,128]{2,1,0:T(8,128)(2,1)S(1)}, u32[]{:S(2)}, u32[]{:S(2)}) collective-permute-start(bf16[2,512,128]{2,1,0:T(8,128)(2,1)S(1)} %bitcast.153), channel_id=1, source_target_pairs={{13,0},{14,1},{15,2},{0,3},{1,4},{2,5},{3,6},{4,7},{5,8},{6,9},{7,... | collective-permute-start | bytes 786440 | tf_op jit(solution)/shard_map/ppermute | solution.py:26
  121.3 83.9 %collective-permute-start.18 = (bf16[2,512,128]{2,1,0:T(8,128)(2,1)S(1)}, bf16[2,512,128]{2,1,0:T(8,128)(2,1)S(1)}, u32[]{:S(2)}, u32[]{:S(2)}) collective-permute-start(bf16[2,512,128]{2,1,0:T(8,128)(2,1)S(1)} %bitcast.152), channel_id=1, source_target_pairs={{12,0},{13,1},{14,2},{15,3},{0,4},{1,5},{2,6},{3,7},{4,8},{5,9},{6... | collective-permute-start | bytes 786440 | tf_op jit(solution)/shard_map/ppermute | solution.py:26
  123.1 82.9 %collective-permute-start.19 = (bf16[2,512,128]{2,1,0:T(8,128)(2,1)S(1)}, bf16[2,512,128]{2,1,0:T(8,128)(2,1)S(1)}, u32[]{:S(2)}, u32[]{:S(2)}) collective-permute-start(bf16[2,512,128]{2,1,0:T(8,128)(2,1)S(1)} %bitcast.151), channel_id=1, source_target_pairs={{11,0},{12,1},{13,2},{14,3},{15,4},{0,5},{1,6},{2,7},{3,8},{4,9},{... | collective-permute-start | bytes 786440 | tf_op jit(solution)/shard_map/ppermute | solution.py:26
  203.0 19.8 %collective-permute-start.20 = (bf16[2,512,128]{2,1,0:T(8,128)(2,1)S(1)}, bf16[2,512,128]{2,1,0:T(8,128)(2,1)S(1)}, u32[]{:S(2)}, u32[]{:S(2)}) collective-permute-start(bf16[2,512,128]{2,1,0:T(8,128)(2,1)S(1)} %bitcast.157), channel_id=1, source_target_pairs={{10,0},{11,1},{12,2},{13,3},{14,4},{15,5},{0,6},{1,7},{2,8},{3,9},... | collective-permute-start | bytes 786440 | tf_op jit(solution)/shard_map/ppermute | solution.py:26
  203.8 19.7 %collective-permute-start.21 = (bf16[2,512,128]{2,1,0:T(8,128)(2,1)S(1)}, bf16[2,512,128]{2,1,0:T(8,128)(2,1)S(1)}, u32[]{:S(2)}, u32[]{:S(2)}) collective-permute-start(bf16[2,512,128]{2,1,0:T(8,128)(2,1)S(1)} %bitcast.156), channel_id=1, source_target_pairs={{9,0},{10,1},{11,2},{12,3},{13,4},{14,5},{15,6},{0,7},{1,8},{2,9},... | collective-permute-start | bytes 786440 | tf_op jit(solution)/shard_map/ppermute | solution.py:26
Sparse Core Ops, SparseCore 0:
  203.1 99.3 all-reduce.3
